TPU v7x, 256 devices: a whole 4x4x8 slice. The times are simulated.
256 devices in a mesh: seq: 32 (over z, y_hi, core), chan: 8 (over y_lo, x).
Axes of the slice: x: 4, y: 4 (y_hi: 2, y_lo: 2; y = y_hi * 2 + y_lo), z: 8, core: 2. Of those that a mesh axis runs over, the one named last changes fastest.
Arguments:
- tokens: bfloat16 [384, 512, 1024], P('chan', 'seq'), may hold values from -6 to 6
- gating: bfloat16 [384, 512, 1024], P(None, ('seq', 'chan')), may hold values from -6 to 6
- kernel: bfloat16 [384, 1024, 512], P('chan', 'seq'), may hold values from -6 to 6
- first_factor: bfloat16 [1024, 1024], replicated, may hold values from -0.1875 to 0.1875
- first_twiddle: float32 [512, 1024], P('seq'), may hold values from 0.5 to 1.5
- second_factor: bfloat16 [512, 512], replicated, may hold values from -0.25 to 0.25
- inverse_second: bfloat16 [512, 512], replicated, may hold values from -0.25 to 0.25
- inverse_twiddle: float32 [1024, 512], P('seq'), may hold values from 0.5 to 1.5
- inverse_first: bfloat16 [1024, 1024], replicated, may hold values from -0.1875 to 0.1875
- projection: bfloat16 [384, 384], replicated, may hold values from -0.3125 to 0.3125
Outputs:
- result: bfloat16 [384, 512, 1024], P(None, ('seq', 'chan'))
All inputs are finite; a program needn't handle non-finite values.
Results may differ from a plain program's by a relative error of at most 0.012.
Values may be sent and summed in bfloat16 or wider, within the bound.
A program may use at most 64 MiB of HBM per device.

v0:
```python
import jax
import jax.numpy as jnp
from jax import lax
from jax.sharding import PartitionSpec as P


def body(
    tokens,
    gating,
    kernel,
    first_factor,
    first_twiddle,
    second_factor,
    inverse_second,
    inverse_twiddle,
    inverse_first,
    projection,
):
    seq_count = lax.axis_size("seq")
    chan_count = lax.axis_size("chan")
    channels, local_rows, order_inner = tokens.shape
    order_outer = second_factor.shape[0]
    block_cols = order_inner // seq_count
    chan_rows = local_rows // chan_count
    first_split = first_factor.reshape(seq_count, block_cols, order_inner)
    forward = jnp.einsum("cab,skb->scka", tokens, first_split, preferred_element_type=jnp.float32)
    twiddle = first_twiddle.reshape(local_rows, seq_count, block_cols).transpose(1, 2, 0)
    forward = (forward * twiddle[:, None]).astype(jnp.bfloat16)
    forward = forward.reshape(seq_count, 1, channels, block_cols * local_rows)
    received = lax.all_to_all(forward, "seq", split_axis=0, concat_axis=1, tiled=True)
    received = received.reshape(seq_count, channels, block_cols, local_rows)
    second_split = second_factor.reshape(order_outer, seq_count, local_rows)
    spectrum = jnp.einsum(
        "scka,jsa->ckj", received, second_split, preferred_element_type=jnp.float32
    )
    scaled = (spectrum * kernel).astype(jnp.bfloat16)
    first_join = inverse_first.reshape(order_inner, seq_count, block_cols)
    inverse_split = inverse_second.reshape(seq_count, local_rows, order_outer)
    inverse = jnp.einsum("ckj,sij->scki", scaled, inverse_split, preferred_element_type=jnp.float32)
    twiddle_back = inverse_twiddle.reshape(block_cols, seq_count, local_rows).transpose(1, 0, 2)
    inverse = (inverse * twiddle_back[:, None]).astype(jnp.bfloat16)
    inverse = inverse.reshape(seq_count, 1, channels, block_cols * local_rows)
    returned = lax.all_to_all(inverse, "seq", split_axis=0, concat_axis=1, tiled=True)
    returned = returned.reshape(seq_count, channels, block_cols, local_rows)
    mixed_rows = jnp.einsum(
        "scki,bsk->cib", returned, first_join, preferred_element_type=jnp.float32
    ).astype(jnp.bfloat16)
    mixed_rows = mixed_rows.reshape(channels, chan_count, chan_rows, order_inner)
    mixed_rows = lax.all_to_all(mixed_rows, "chan", split_axis=1, concat_axis=0, tiled=True)
    mixed_rows = mixed_rows.reshape(channels * chan_count, chan_rows, order_inner)
    gated_rows = (mixed_rows.astype(jnp.float32) * gating.astype(jnp.float32)).astype(jnp.bfloat16)
    result_rows = jnp.einsum(
        "cab,ce->eab", gated_rows, projection, preferred_element_type=jnp.float32
    )
    return result_rows.astype(jnp.bfloat16)


def solution(mesh):
    return jax.shard_map(
        body,
        mesh=mesh,
        in_specs=(
            P("chan", "seq", None),
            P(None, ("seq", "chan"), None),
            P("chan", "seq", None),
            P(),
            P("seq", None),
            P(),
            P(),
            P("seq", None),
            P(),
            P(),
        ),
        out_specs=P(None, ("seq", "chan"), None),
        check_vma=False,
    )
```

profile of v0, /device:TPU:16, one launch (start us, length us, event | category | flops | bytes accessed | tf_op | source)
XLA Modules:
  0.0 208.6 jit_solution(16965171331436541552)
XLA Ops:
  0.0 1.1 reshape.50
  1.3 0.3 copy-done
  1.6 6.3 %fusion.1 = bf16[32,48,32,16]{1,2,3,0:T(8,128)(2,1)S(1)} fusion(f32[32,32,16]{1,2,0:T(8,128)S(1)} %bitcast.80, bf16[32,32,1024,1]{2,1,3,0:T(8,128)(2,1)S(1)} %bitcast.72, bf16[48,16,1024]{2,1,0:T(8,128)(2,1)} %param.10), kind=kOutput, calls=%fused_computation.3 | convolution fusion | flops 1612185600 | bytes 5308416 | tf_op jit(solution)/shard_map/cab,skb->scka/dot_general | solution.py:26
  8.0 3.9 %copy.35 = bf16[32,48,32,16]{1,3,2,0:T(8,128)(2,1)} copy(bf16[32,48,32,16]{1,2,3,0:T(8,128)(2,1)S(1)} %fusion.1) | data formatting | bytes 3145728 | tf_op jit(solution)/shard_map/convert_element_type | solution.py:28
  11.9 4.7 %copy.36 = bf16[32,1,48,512]{3,2,1,0:T(8,128)(2,1)} copy(bf16[32,1,48,512]{2,3,0,1:T(8,128)(2,1)} %bitcast.73) | data formatting | bytes 3145728 | tf_op jit(solution)/shard_map/reshape | solution.py:29
  16.5 11.7 %all-to-all-start = ((bf16[32,1,48,512]{3,2,1,0:T(8,128)(2,1)}), bf16[32,1,48,512]{3,2,1,0:T(8,128)(2,1)S(1)}, u32[]{:S(2)}, u32[]{:S(2)}) async-start(bf16[32,1,48,512]{3,2,1,0:T(8,128)(2,1)} %copy.36), calls=%async_computation | async-start | bytes 3145728 | tf_op jit(solution)/shard_map/all_to_all | solution.py:30
  28.8 38.6 %all-to-all-done = bf16[32,1,48,512]{3,2,1,0:T(8,128)(2,1)S(1)} async-done(((bf16[32,1,48,512]{3,2,1,0:T(8,128)(2,1)}), bf16[32,1,48,512]{3,2,1,0:T(8,128)(2,1)S(1)}, u32[]{:S(2)}, u32[]{:S(2)}) %all-to-all-start) | async-done | bytes 1572896 | tf_op jit(solution)/shard_map/all_to_all | solution.py:30
  67.4 3.2 %copy.37 = bf16[32,1,48,512]{2,3,0,1:T(8,128)(2,1)} copy(bf16[32,1,48,512]{3,2,1,0:T(8,128)(2,1)S(1)} %all-to-all-done) | data formatting | bytes 3145728 | tf_op jit(solution)/shard_map/all_to_all | solution.py:30
  70.6 12.8 %copy.39 = bf16[32,48,32,16]{2,3,0,1:T(8,128)(2,1)} copy(bf16[32,48,32,16]{1,3,2,0:T(8,128)(2,1)} %bitcast.74) | data formatting | bytes 3145728 | tf_op jit(solution)/shard_map/reshape | solution.py:31
  83.3 9.0 %fusion = bf16[32,48,32,16]{0,2,3,1:T(8,128)(2,1)} fusion(f32[32,32,16]{0,1,2:T(8,128)S(1)} %copy.42, bf16[48,32,512]{2,1,0:T(8,128)(2,1)S(1)} %copy-done.5, bf16[32,48,32,16]{2,3,0,1:T(8,128)(2,1)} %copy.39, bf16[512,32,16,1]{0,2,1,3:T(8,128)(2,1)S(1)} %bitcast.79, bf16[32,16,512]{2,1,0:T(8,128)(2,1)S(1)} %bitcast.81), kind=kOutput, calls=%fused_computation.1 | convolution fusion | flops 1614544896 | bytes 5832704 | tf_op jit(solution)/shard_map/ckj,sij->scki/dot_general | solution.py:39
  92.3 12.7 %copy.43 = bf16[32,48,32,16]{1,3,2,0:T(8,128)(2,1)} copy(bf16[32,48,32,16]{0,2,3,1:T(8,128)(2,1)} %fusion) | data formatting | bytes 3145728 | tf_op jit(solution)/shard_map/convert_element_type | solution.py:41
  105.1 4.7 %copy.44 = bf16[32,1,48,512]{3,2,1,0:T(8,128)(2,1)} copy(bf16[32,1,48,512]{2,3,0,1:T(8,128)(2,1)} %bitcast.75) | data formatting | bytes 3145728 | tf_op jit(solution)/shard_map/reshape | solution.py:42
  109.7 6.0 %all-to-all-start.1 = ((bf16[32,1,48,512]{3,2,1,0:T(8,128)(2,1)}), bf16[32,1,48,512]{3,2,1,0:T(8,128)(2,1)S(1)}, u32[]{:S(2)}, u32[]{:S(2)}) async-start(bf16[32,1,48,512]{3,2,1,0:T(8,128)(2,1)} %copy.44), calls=%async_computation.1 | async-start | bytes 3145728 | tf_op jit(solution)/shard_map/all_to_all | solution.py:43
  115.7 4.0 %copy.46 = bf16[1024,1024]{0,1:T(8,128)(2,1)} copy(bf16[1024,1024]{1,0:T(8,128)(2,1)} %param.18) | data formatting | bytes 4194304 | tf_op args[8]
  119.7 35.1 %all-to-all-done.1 = bf16[32,1,48,512]{3,2,1,0:T(8,128)(2,1)S(1)} async-done(((bf16[32,1,48,512]{3,2,1,0:T(8,128)(2,1)}), bf16[32,1,48,512]{3,2,1,0:T(8,128)(2,1)S(1)}, u32[]{:S(2)}, u32[]{:S(2)}) %all-to-all-start.1) | async-done | bytes 1572896 | tf_op jit(solution)/shard_map/all_to_all | solution.py:43
  154.9 4.7 %copy.45 = bf16[32,1,48,512]{0,3,2,1:T(8,128)(2,1)} copy(bf16[32,1,48,512]{3,2,1,0:T(8,128)(2,1)S(1)} %all-to-all-done.1) | data formatting | bytes 3145728 | tf_op jit(solution)/shard_map/all_to_all | solution.py:43
  159.5 8.5 %bitcast_convert_fusion = bf16[48,16,1024]{2,1,0:T(8,128)(2,1)} fusion(bf16[32,48,32,16]{0,3,2,1:T(8,128)(2,1)} %bitcast.76, bf16[1024,32,32]{0,2,1:T(8,128)(2,1)} %bitcast.77), kind=kOutput, calls=%fused_computation.6 | convolution fusion | flops 1611399168 | bytes 5242880 | tf_op jit(solution)/shard_map/scki,bsk->cib/dot_general | solution.py:45
  168.1 2.5 %reshape.59 = bf16[48,8,2,1024]{3,2,1,0:T(2,128)(2,1)S(1)} reshape(bf16[48,16,1024]{2,1,0:T(8,128)(2,1)} %bitcast_convert_fusion) | data formatting | bytes 3145728 | tf_op jit(solution)/shard_map/reshape | solution.py:48
  170.6 1.1 copy.48
  171.7 26.3 %all_to_all.12 = bf16[48,8,2,1024]{3,2,0,1:T(2,128)(2,1)S(1)} all-to-all(bf16[48,8,2,1024]{3,2,0,1:T(2,128)(2,1)S(1)} %copy.48), channel_id=1, replica_groups=mesh['seq'=32,'chan'=8] {'chan'}, dimensions={1} | all-to-all | bytes 3145728 | tf_op jit(solution)/shard_map/all_to_all | solution.py:49
  198.0 1.1 bitcast_convert_fusion.1
  199.4 1.9 fusion.2
  201.4 2.3 %fusion.13 = bf16[384,2,1024]{0,2,1:T(8,128)(2,1)} fusion(bf16[384,2,1024]{2,1,0:T(2,128)(2,1)S(1)} %fusion.2, bf16[384,384]{1,0:T(8,128)(2,1)S(1)} %copy-done.7), kind=kOutput, calls=%fused_computation.18 | convolution fusion | flops 604766208 | bytes 3440640 | tf_op jit(solution)/shard_map/cab,ce->eab/dot_general | solution.py:52
  203.7 4.9 %copy.50 = bf16[384,2,1024]{2,1,0:T(2,128)(2,1)} copy(bf16[384,2,1024]{0,2,1:T(8,128)(2,1)} %fusion.13) | data formatting | bytes 3145728 | tf_op jit(solution)/shard_map/convert_element_type | solution.py:55
  (19 shorter events, 1.0 us)
Async XLA Ops:
  0.0 1.6 copy-start
  16.5 11.7 %copy-start.3 = (bf16[512,512]{1,0:T(8,128)(2,1)S(1)}, bf16[512,512]{1,0:T(8,128)(2,1)}, u32[]{:S(2)}) copy-start(bf16[512,512]{1,0:T(8,128)(2,1)} %param.15) | copy-start | bytes 1572868
  16.5 12.0 %copy-start.4 = (f32[32,512]{1,0:T(8,128)S(1)}, f32[32,512]{1,0:T(8,128)}, u32[]{:S(2)}) copy-start(f32[32,512]{1,0:T(8,128)} %param.17) | copy-start | bytes 196612
  16.5 50.9 %all-to-all-start = ((bf16[32,1,48,512]{3,2,1,0:T(8,128)(2,1)}), bf16[32,1,48,512]{3,2,1,0:T(8,128)(2,1)S(1)}, u32[]{:S(2)}, u32[]{:S(2)}) async-start(bf16[32,1,48,512]{3,2,1,0:T(8,128)(2,1)} %copy.36), calls=%async_computation | async-start | bytes 3145728 | tf_op jit(solution)/shard_map/all_to_all | solution.py:30
  70.6 12.8 %copy-start.5 = (bf16[48,32,512]{2,1,0:T(8,128)(2,1)S(1)}, bf16[48,32,512]{2,1,0:T(8,128)(2,1)}, u32[]{:S(2)}) copy-start(bf16[48,32,512]{2,1,0:T(8,128)(2,1)} %param.12) | copy-start | bytes 4718596
  70.6 12.8 %copy-start.6 = (bf16[512,512]{1,0:T(8,128)(2,1)S(1)}, bf16[512,512]{1,0:T(8,128)(2,1)}, u32[]{:S(2)}) copy-start(bf16[512,512]{1,0:T(8,128)(2,1)} %param.16) | copy-start | bytes 1572868
  109.7 45.1 %all-to-all-start.1 = ((bf16[32,1,48,512]{3,2,1,0:T(8,128)(2,1)}), bf16[32,1,48,512]{3,2,1,0:T(8,128)(2,1)S(1)}, u32[]{:S(2)}, u32[]{:S(2)}) async-start(bf16[32,1,48,512]{3,2,1,0:T(8,128)(2,1)} %copy.44), calls=%async_computation.1 | async-start | bytes 3145728 | tf_op jit(solution)/shard_map/all_to_all | solution.py:43
  198.0 1.4 copy-start.2
  199.4 1.9 copy-start.7
  201.3 7.3 %copy-start.1 = (bf16[1024,1024]{1,0:T(8,128)(2,1)S(1)}, bf16[1024,1024]{1,0:T(8,128)(2,1)}, u32[]{:S(2)}) copy-start(bf16[1024,1024]{1,0:T(8,128)(2,1)} %param.13) | copy-start | bytes 6291460
where the time goes:
time: 210 us; the launch traced here: 209 us
  waiting for transfers between devices  73.8 us (35%)
  local copies, waits for them, and re-layouts  61.5 us (29%)
  blocking collectives  26.3 us (13%)
  matrix products  26.2 us (12%)
  starting transfers between devices  17.7 us (8%)
  other arithmetic  3 us (1%)
    all_to_all x1, waiting for transfers between devices, body(): lax.all_to_all(forward, 'seq', split_axis=0, concat_axis=1, tiled=True)  38.6 us
    all_to_all x1, waiting for transfers between devices, body(): lax.all_to_all(inverse, 'seq', split_axis=0, concat_axis=1, tiled=True)  35.1 us
    all_to_all x1, blocking collectives, body(): lax.all_to_all(mixed_rows, 'chan', split_axis=1, concat_axis=0, tiled=True)  26.3 us
    reshape x1, local copies, waits for them, and re-layouts, body(): received = received.reshape(seq_count, channels, block_cols, local_rows)  12.8 us
    convert_element_type x1, local copies, waits for them, and re-layouts, body(): inverse = (inverse * twiddle_back[:, None]).astype(jnp.bfloat16)  12.7 us
    all_to_all x1, starting transfers between devices, body(): lax.all_to_all(forward, 'seq', split_axis=0, concat_axis=1, tiled=True)  11.7 us
    dot_general x1, matrix products, body(): jnp.einsum('ckj,sij->scki', scaled, inverse_split, preferred_element_type...  8.99 us
    dot_general x1, matrix products, body(): jnp.einsum('scki,bsk->cib', returned, first_join, preferred_element_type=...  8.55 us
  transfers between devices with their start and end apart: 2, of which 2 were waited for; matrix products, arithmetic and copies ran while one was open for 2% of the time, Pallas kernels for 0%

commit v1 on v0

--- a/solution.py
+++ b/solution.py
@@ -40,7 +40,9 @@
     twiddle_back = inverse_twiddle.reshape(block_cols, seq_count, local_rows).transpose(1, 0, 2)
     inverse = (inverse * twiddle_back[:, None]).astype(jnp.bfloat16)
     inverse = inverse.reshape(seq_count, 1, channels, block_cols * local_rows)
-    returned = lax.all_to_all(inverse, "seq", split_axis=0, concat_axis=1, tiled=True)
+    pieces = jnp.split(inverse, lax.axis_size("seq"), axis=0)
+    incoming = lax.all_to_all(jnp.stack(pieces), "seq", 0, 0)
+    returned = jnp.concatenate(incoming, axis=1)
     returned = returned.reshape(seq_count, channels, block_cols, local_rows)
     mixed_rows = jnp.einsum(
         "scki,bsk->cib", returned, first_join, preferred_element_type=jnp.float32

time: 210 us -> 261 us (1.24)
  local copies, waits for them, and re-layouts: 61.5 us -> 112 us
    split x0 -> x34, local copies, waits for them, and re-layouts: none -> 40.1 us  [body(): pieces = jnp.split(inverse, lax.axis_size('seq'), axis=0)]
    unnamed x19 -> x104, local copies, waits for them, and re-layouts: 5.01 us -> 24.4 us
    convert_element_type x1 -> x0, local copies, waits for them, and re-layouts: 12.7 us -> none  [body(): inverse = (inverse * twiddle_back[:, None]).astype(jnp.bfloat16)]
    another operation x0 -> x33, local copies, waits for them, and re-layouts: none -> 8.55 us  [body(): incoming = lax.all_to_all(jnp.stack(pieces), 'seq', 0, 0)]
    reshape x1 -> x0, local copies, waits for them, and re-layouts: 4.66 us -> none  [body(): inverse = inverse.reshape(seq_count, 1, channels, block_cols * local_rows)]
where the time goes in v1:
time: 261 us; the launch traced here: 260 us
  local copies, waits for them, and re-layouts  112 us (43%)
  waiting for transfers between devices  73.9 us (28%)
  matrix products  26.3 us (10%)
  blocking collectives  26.3 us (10%)
  starting transfers between devices  17.7 us (7%)
  other arithmetic  3 us (1%)
    split x34, local copies, waits for them, and re-layouts, body(): pieces = jnp.split(inverse, lax.axis_size('seq'), axis=0)  40.1 us
    all_to_all x1, waiting for transfers between devices, body(): lax.all_to_all(forward, 'seq', split_axis=0, concat_axis=1, tiled=True)  38.7 us
    all_to_all x1, waiting for transfers between devices, body(): incoming = lax.all_to_all(jnp.stack(pieces), 'seq', 0, 0)  35.2 us
    all_to_all x1, blocking collectives, body(): lax.all_to_all(mixed_rows, 'chan', split_axis=1, concat_axis=0, tiled=True)  26.3 us
    unnamed x104, local copies, waits for them, and re-layouts  24.4 us
    reshape x1, local copies, waits for them, and re-layouts, body(): received = received.reshape(seq_count, channels, block_cols, local_rows)  12.8 us
    all_to_all x1, starting transfers between devices, body(): lax.all_to_all(forward, 'seq', split_axis=0, concat_axis=1, tiled=True)  11.7 us
    dot_general x1, matrix products, body(): jnp.einsum('ckj,sij->scki', scaled, inverse_split, preferred_element_type...  9 us
  transfers between devices with their start and end apart: 2, of which 2 were waited for; matrix products, arithmetic and copies ran while one was open for 2% of the time, Pallas kernels for 0%

profile of v1, /device:TPU:16, one launch (start us, length us, event | category | flops | bytes accessed | tf_op | source)
XLA Modules:
  0.0 260.1 jit_solution(13782792696622776411)
XLA Ops:
  1.6 6.3 %fusion.1 = bf16[32,48,32,16]{1,2,3,0:T(8,128)(2,1)S(1)} fusion(f32[32,32,16]{1,2,0:T(8,128)S(1)} %bitcast.142, bf16[32,32,1024,1]{2,1,3,0:T(8,128)(2,1)S(1)} %bitcast.103, bf16[48,16,1024]{2,1,0:T(8,128)(2,1)} %param.10), kind=kOutput, calls=%fused_computation.3 | convolution fusion | flops 1612185600 | bytes 5308416 | tf_op jit(solution)/shard_map/cab,skb->scka/dot_general | solution.py:26
  8.0 3.9 %copy.66 = bf16[32,48,32,16]{1,3,2,0:T(8,128)(2,1)} copy(bf16[32,48,32,16]{1,2,3,0:T(8,128)(2,1)S(1)} %fusion.1) | data formatting | bytes 3145728 | tf_op jit(solution)/shard_map/convert_element_type | solution.py:28
  11.9 4.7 %copy.67 = bf16[32,1,48,512]{3,2,1,0:T(8,128)(2,1)} copy(bf16[32,1,48,512]{2,3,0,1:T(8,128)(2,1)} %bitcast.104) | data formatting | bytes 3145728 | tf_op jit(solution)/shard_map/reshape | solution.py:29
  16.6 11.7 %all-to-all-start = ((bf16[32,1,48,512]{3,2,1,0:T(8,128)(2,1)}), bf16[32,1,48,512]{3,2,1,0:T(8,128)(2,1)S(1)}, u32[]{:S(2)}, u32[]{:S(2)}) async-start(bf16[32,1,48,512]{3,2,1,0:T(8,128)(2,1)} %copy.67), calls=%async_computation | async-start | bytes 3145728 | tf_op jit(solution)/shard_map/all_to_all | solution.py:30
  28.8 38.7 %all-to-all-done = bf16[32,1,48,512]{3,2,1,0:T(8,128)(2,1)S(1)} async-done(((bf16[32,1,48,512]{3,2,1,0:T(8,128)(2,1)}), bf16[32,1,48,512]{3,2,1,0:T(8,128)(2,1)S(1)}, u32[]{:S(2)}, u32[]{:S(2)}) %all-to-all-start) | async-done | bytes 1572896 | tf_op jit(solution)/shard_map/all_to_all | solution.py:30
  67.4 3.1 %copy.68 = bf16[32,1,48,512]{2,3,0,1:T(8,128)(2,1)} copy(bf16[32,1,48,512]{3,2,1,0:T(8,128)(2,1)S(1)} %all-to-all-done) | data formatting | bytes 3145728 | tf_op jit(solution)/shard_map/all_to_all | solution.py:30
  70.6 12.8 %copy.70 = bf16[32,48,32,16]{2,3,0,1:T(8,128)(2,1)} copy(bf16[32,48,32,16]{1,3,2,0:T(8,128)(2,1)} %bitcast.105) | data formatting | bytes 3145728 | tf_op jit(solution)/shard_map/reshape | solution.py:31
  83.3 9.0 %fusion = bf16[32,48,32,16]{2,0,3,1:T(8,128)(2,1)} fusion(f32[32,32,16]{1,0,2:T(8,128)S(1)} %copy.73, bf16[48,32,512]{2,1,0:T(8,128)(2,1)S(1)} %copy-done.32, bf16[32,48,32,16]{2,3,0,1:T(8,128)(2,1)} %copy.70, bf16[512,32,16,1]{0,2,1,3:T(8,128)(2,1)S(1)} %bitcast.109, bf16[32,16,512]{2,1,0:T(8,128)(2,1)S(1)} %bitcast.143), kind=kOutput, calls=%fused_computation.1 | convolution fusion | flops 1614544896 | bytes 5832704 | tf_op jit(solution)/shard_map/ckj,sij->scki/dot_general | solution.py:39
  92.3 12.6 %fusion.20 = (bf16[1,48,32,16]{2,0,3,1:T(2,128)(2,1)S(1)}, bf16[1,48,32,16]{2,0,3,1:T(2,128)(2,1)S(1)}, bf16[1,48,32,16]{2,0,3,1:T(2,128)(2,1)S(1)}, bf16[1,48,3...) fusion(bf16[32,48,32,16]{2,0,3,1:T(8,128)(2,1)} %fusion), kind=kLoop, calls=%fused_computation.56 | loop fusion | bytes 1277952 | tf_op jit(solution)/shard_map/split | solution.py:43
  104.9 8.4 %fusion.19 = (bf16[1,48,32,16]{2,0,3,1:T(2,128)(2,1)}, bf16[1,48,32,16]{2,0,3,1:T(2,128)(2,1)}, bf16[1,48,32,16]{2,0,3,1:T(2,128)(2,1)}, bf16[1,48,32,16]{2,0,3,...) fusion(bf16[32,48,32,16]{2,0,3,1:T(8,128)(2,1)S(1)} %copy-done.2), kind=kLoop, calls=%fused_computation.55 | loop fusion | bytes 1867776 | tf_op jit(solution)/shard_map/split | solution.py:43
  113.4 1.3 copy.74
  116.8 1.3 copy.76
  118.2 1.3 copy.77
  119.6 1.3 copy.78
  161.2 6.0 %all-to-all-start.1 = ((bf16[32,1,1,48,512]{4,3,2,1,0:T(8,128)(2,1)}), bf16[32,1,1,48,512]{4,3,2,1,0:T(8,128)(2,1)S(1)}, u32[]{:S(2)}, u32[]{:S(2)}) async-start(bf16[32,1,1,48,512]{4,3,2,1,0:T(8,128)(2,1)} %constant_dynamic-update-slice_fusion), calls=%async_computation.1 | async-start | bytes 3145728 | tf_op jit(solution)/shard_map/all_to_all | solution.py:44
  167.2 4.0 %copy.139 = bf16[1024,1024]{0,1:T(8,128)(2,1)} copy(bf16[1024,1024]{1,0:T(8,128)(2,1)} %param.18) | data formatting | bytes 4194304 | tf_op args[8]
  171.2 35.2 %all-to-all-done.1 = bf16[32,1,1,48,512]{4,3,2,1,0:T(8,128)(2,1)S(1)} async-done(((bf16[32,1,1,48,512]{4,3,2,1,0:T(8,128)(2,1)}), bf16[32,1,1,48,512]{4,3,2,1,0:T(8,128)(2,1)S(1)}, u32[]{:S(2)}, u32[]{:S(2)}) %all-to-all-start.1) | async-done | bytes 1572896 | tf_op jit(solution)/shard_map/all_to_all | solution.py:44
  206.3 4.7 %copy.138 = bf16[32,1,1,48,512]{0,4,3,2,1:T(8,128)(2,1)} copy(bf16[32,1,1,48,512]{4,3,2,1,0:T(8,128)(2,1)S(1)} %all-to-all-done.1) | data formatting | bytes 3145728 | tf_op jit(solution)/shard_map/all_to_all | solution.py:44
  211.0 8.5 %bitcast_convert_fusion = bf16[48,16,1024]{2,1,0:T(8,128)(2,1)} fusion(bf16[32,48,32,16]{0,3,2,1:T(8,128)(2,1)} %bitcast.106, bf16[1024,32,32]{0,2,1:T(8,128)(2,1)} %bitcast.107), kind=kOutput, calls=%fused_computation.6 | convolution fusion | flops 1611399168 | bytes 5242880 | tf_op jit(solution)/shard_map/scki,bsk->cib/dot_general | solution.py:47
  219.6 2.5 reshape.112
  223.2 26.3 %all_to_all.23 = bf16[48,8,2,1024]{3,2,0,1:T(2,128)(2,1)S(1)} all-to-all(bf16[48,8,2,1024]{3,2,0,1:T(2,128)(2,1)S(1)} %copy.141), channel_id=1, replica_groups=mesh['seq'=32,'chan'=8] {'chan'}, dimensions={1} | all-to-all | bytes 3145728 | tf_op jit(solution)/shard_map/all_to_all | solution.py:51
  250.9 1.9 fusion.2
  252.8 2.4 fusion.13
  255.2 4.9 %copy.143 = bf16[384,2,1024]{2,1,0:T(2,128)(2,1)} copy(bf16[384,2,1024]{0,2,1:T(8,128)(2,1)} %fusion.13) | data formatting | bytes 3145728 | tf_op jit(solution)/shard_map/convert_element_type | solution.py:57
  (169 shorter events, 46.4 us)
Async XLA Ops:
  16.5 11.7 %copy-start.22 = (bf16[512,512]{1,0:T(8,128)(2,1)S(1)}, bf16[512,512]{1,0:T(8,128)(2,1)}, u32[]{:S(2)}) copy-start(bf16[512,512]{1,0:T(8,128)(2,1)} %param.15) | copy-start | bytes 1572868
  16.6 12.0 %copy-start.31 = (f32[32,512]{1,0:T(8,128)S(1)}, f32[32,512]{1,0:T(8,128)}, u32[]{:S(2)}) copy-start(f32[32,512]{1,0:T(8,128)} %param.17) | copy-start | bytes 196612
  16.6 50.9 %all-to-all-start = ((bf16[32,1,48,512]{3,2,1,0:T(8,128)(2,1)}), bf16[32,1,48,512]{3,2,1,0:T(8,128)(2,1)S(1)}, u32[]{:S(2)}, u32[]{:S(2)}) async-start(bf16[32,1,48,512]{3,2,1,0:T(8,128)(2,1)} %copy.67), calls=%async_computation | async-start | bytes 3145728 | tf_op jit(solution)/shard_map/all_to_all | solution.py:30
  70.6 12.8 %copy-start.32 = (bf16[48,32,512]{2,1,0:T(8,128)(2,1)S(1)}, bf16[48,32,512]{2,1,0:T(8,128)(2,1)}, u32[]{:S(2)}) copy-start(bf16[48,32,512]{2,1,0:T(8,128)(2,1)} %param.12) | copy-start | bytes 4718596
  70.6 12.8 %copy-start.33 = (bf16[512,512]{1,0:T(8,128)(2,1)S(1)}, bf16[512,512]{1,0:T(8,128)(2,1)}, u32[]{:S(2)}) copy-start(bf16[512,512]{1,0:T(8,128)(2,1)} %param.16) | copy-start | bytes 1572868
  92.3 12.6 %copy-start.2 = (bf16[32,48,32,16]{2,0,3,1:T(8,128)(2,1)S(1)}, bf16[32,48,32,16]{2,0,3,1:T(8,128)(2,1)}, u32[]{:S(2)}) copy-start(bf16[32,48,32,16]{2,0,3,1:T(8,128)(2,1)} %fusion) | copy-start | bytes 4718596
  125.4 6.2 %copy-start.21 = (bf16[1,48,32,16]{2,0,3,1:T(2,128)(2,1)S(1)}, bf16[1,48,32,16]{2,0,3,1:T(2,128)(2,1)}, u32[]{:S(2)}) copy-start(bf16[1,48,32,16]{2,0,3,1:T(2,128)(2,1)} %get-tuple-element.22) | copy-start | bytes 147460
  126.6 5.6 %copy-start.20 = (bf16[1,48,32,16]{2,0,3,1:T(2,128)(2,1)S(1)}, bf16[1,48,32,16]{2,0,3,1:T(2,128)(2,1)}, u32[]{:S(2)}) copy-start(bf16[1,48,32,16]{2,0,3,1:T(2,128)(2,1)} %get-tuple-element.21) | copy-start | bytes 147460
  127.7 5.2 %copy-start.19 = (bf16[1,48,32,16]{2,0,3,1:T(2,128)(2,1)S(1)}, bf16[1,48,32,16]{2,0,3,1:T(2,128)(2,1)}, u32[]{:S(2)}) copy-start(bf16[1,48,32,16]{2,0,3,1:T(2,128)(2,1)} %get-tuple-element.20) | copy-start | bytes 147460
  128.9 4.6 %copy-start.18 = (bf16[1,48,32,16]{2,0,3,1:T(2,128)(2,1)S(1)}, bf16[1,48,32,16]{2,0,3,1:T(2,128)(2,1)}, u32[]{:S(2)}) copy-start(bf16[1,48,32,16]{2,0,3,1:T(2,128)(2,1)} %get-tuple-element.19) | copy-start | bytes 147460
  130.9 3.1 %copy-start.17 = (bf16[1,48,32,16]{2,0,3,1:T(2,128)(2,1)S(1)}, bf16[1,48,32,16]{2,0,3,1:T(2,128)(2,1)}, u32[]{:S(2)}) copy-start(bf16[1,48,32,16]{2,0,3,1:T(2,128)(2,1)} %get-tuple-element.18) | copy-start | bytes 147460
  132.1 2.5 copy-start.16
  137.8 2.4 copy-start.6
  138.4 2.4 copy-start.5
  139.6 5.4 %copy-start.23 = (bf16[1,1,1,48,512]{4,3,2,1,0:T(8,128)(2,1)S(1)}, bf16[1,1,1,48,512]{4,3,2,1,0:T(8,128)(2,1)}, u32[]{:S(2)}) copy-start(bf16[1,1,1,48,512]{4,3,2,1,0:T(8,128)(2,1)} %copy.112) | copy-start | bytes 147460
  140.0 5.6 %copy-start.24 = (bf16[1,1,1,48,512]{4,3,2,1,0:T(8,128)(2,1)S(1)}, bf16[1,1,1,48,512]{4,3,2,1,0:T(8,128)(2,1)}, u32[]{:S(2)}) copy-start(bf16[1,1,1,48,512]{4,3,2,1,0:T(8,128)(2,1)} %copy.113) | copy-start | bytes 147460
  140.0 6.2 %copy-start.25 = (bf16[1,1,1,48,512]{4,3,2,1,0:T(8,128)(2,1)S(1)}, bf16[1,1,1,48,512]{4,3,2,1,0:T(8,128)(2,1)}, u32[]{:S(2)}) copy-start(bf16[1,1,1,48,512]{4,3,2,1,0:T(8,128)(2,1)} %copy.114) | copy-start | bytes 147460
  140.1 6.8 %copy-start.26 = (bf16[1,1,1,48,512]{4,3,2,1,0:T(8,128)(2,1)S(1)}, bf16[1,1,1,48,512]{4,3,2,1,0:T(8,128)(2,1)}, u32[]{:S(2)}) copy-start(bf16[1,1,1,48,512]{4,3,2,1,0:T(8,128)(2,1)} %copy.115) | copy-start | bytes 147460
  140.1 7.4 %copy-start.27 = (bf16[1,1,1,48,512]{4,3,2,1,0:T(8,128)(2,1)S(1)}, bf16[1,1,1,48,512]{4,3,2,1,0:T(8,128)(2,1)}, u32[]{:S(2)}) copy-start(bf16[1,1,1,48,512]{4,3,2,1,0:T(8,128)(2,1)} %copy.116) | copy-start | bytes 147460
  140.2 7.9 %copy-start.28 = (bf16[1,1,1,48,512]{4,3,2,1,0:T(8,128)(2,1)S(1)}, bf16[1,1,1,48,512]{4,3,2,1,0:T(8,128)(2,1)}, u32[]{:S(2)}) copy-start(bf16[1,1,1,48,512]{4,3,2,1,0:T(8,128)(2,1)} %copy.117) | copy-start | bytes 147460
  140.2 8.5 %copy-start.29 = (bf16[1,1,1,48,512]{4,3,2,1,0:T(8,128)(2,1)S(1)}, bf16[1,1,1,48,512]{4,3,2,1,0:T(8,128)(2,1)}, u32[]{:S(2)}) copy-start(bf16[1,1,1,48,512]{4,3,2,1,0:T(8,128)(2,1)} %copy.118) | copy-start | bytes 147460
  140.2 9.1 %copy-start.30 = (bf16[1,1,1,48,512]{4,3,2,1,0:T(8,128)(2,1)S(1)}, bf16[1,1,1,48,512]{4,3,2,1,0:T(8,128)(2,1)}, u32[]{:S(2)}) copy-start(bf16[1,1,1,48,512]{4,3,2,1,0:T(8,128)(2,1)} %copy.119) | copy-start | bytes 147460
  161.2 45.1 %all-to-all-start.1 = ((bf16[32,1,1,48,512]{4,3,2,1,0:T(8,128)(2,1)}), bf16[32,1,1,48,512]{4,3,2,1,0:T(8,128)(2,1)S(1)}, u32[]{:S(2)}, u32[]{:S(2)}) async-start(bf16[32,1,1,48,512]{4,3,2,1,0:T(8,128)(2,1)} %constant_dynamic-update-slice_fusion), calls=%async_computation.1 | async-start | bytes 3145728 | tf_op jit(solution)/shard_map/all_to_all | solution.py:44
  252.8 7.3 %copy-start.1 = (bf16[1024,1024]{1,0:T(8,128)(2,1)S(1)}, bf16[1024,1024]{1,0:T(8,128)(2,1)}, u32[]{:S(2)}) copy-start(bf16[1024,1024]{1,0:T(8,128)(2,1)} %param.13) | copy-start | bytes 6291460
  (13 other events, 28.2 us)
